TPU v7x, 512 devices: a whole 4x4x16 slice. The times are simulated.
512 devices in a mesh: head: 8 (over x, core), shard: 64 (over y, z).
Axes of the slice: x: 4, y: 4, z: 16, core: 2. Of those that a mesh axis runs over, the one named last changes fastest.
Arguments:
- tokens: bfloat16 [256, 64, 1024], P('shard'), may hold values from -6 to 6
- w_query: bfloat16 [1024, 1024], P(None, 'head'), may hold values from -0.1875 to 0.1875
- w_key: bfloat16 [1024, 1024], P(None, 'head'), may hold values from -0.1875 to 0.1875
- w_value: bfloat16 [1024, 1024], P(None, 'head'), may hold values from -0.1875 to 0.1875
- w_out: bfloat16 [1024, 1024], P('head'), may hold values from -0.1875 to 0.1875
- norm1_gain: float32 [1024], replicated, may hold values from 0.1 to 1.9
- w_inner: bfloat16 [1024, 4096], P(None, 'head'), may hold values from -0.1875 to 0.1875
- w_outer: bfloat16 [4096, 1024], P('head'), may hold values from -0.09375 to 0.09375
- norm2_gain: float32 [1024], replicated, may hold values from 0.1 to 1.9
- w_project: bfloat16 [1024, 128], replicated, may hold values from -0.1875 to 0.1875
- key_pages: bfloat16 [128, 64, 1024], P('shard', None, 'head'), may hold values from -400 to 400
- value_pages: bfloat16 [128, 64, 1024], P('shard', None, 'head'), may hold values from -6 to 6
- page_table: int32 [128], replicated, may hold values from 0 to 127, as said below
- prompt_lengths: int32 [16], replicated, may hold values from 1 to 512
- request_group: int32 [256], P('shard'), may hold values from 0 to 15, as said below
- doc_vectors: bfloat16 [131072, 128], P(('head', 'shard')), may hold values from -0.29882812 to 0.29882812
- doc_lengths: int32 [512, 4], P(('head', 'shard')), may hold values from 1 to 128, 256 in all within a row
- candidates: int32 [256, 16], P('shard'), may hold values from 0 to 2047, as said below
Outputs:
- embedded: bfloat16 [256, 64, 128], P('shard')
- scores: float32 [256, 16], P('shard')
Inputs may be any that keep to these rules, and one draw needn't show every extreme that they name: `page_table`: positions g * 8 to g * 8 + 7 list the pages of group g's prompt in order; they are the pages g * 8 to g * 8 + 7 in some order. `request_group`: every group has exactly 16 requests; the 4 requests of one index of shard belong to distinct groups. `candidates`: document d is held by the device of index d // 4 along head+shard. `doc_lengths`: each row holds the token counts of one holder's documents in the order they are packed; a row sums to 256.
All inputs are finite; a program needn't handle non-finite values.
Results may differ from a plain program's by a relative error of at most 0.023.
Values may be sent and summed in bfloat16 or wider, within the bound.
No kernel may reach another device: no remote copies, remote signals or barrier semaphores. Data moves between devices by JAX's collectives and lax.ppermute only.
A program may use at most 64 MiB of HBM per device.

v0:
```python
import math
import jax
import jax.numpy as jnp
from jax import lax
from jax.sharding import PartitionSpec as P

DH = 64
PPG = 8
DLMAX = 128


def layer_norm(values, norm_gain):
    row_mean = jnp.mean(values, axis=-1, keepdims=True)
    row_var = jnp.mean(jnp.square(values - row_mean), axis=-1, keepdims=True)
    return (values - row_mean) * lax.rsqrt(row_var + 1e-05) * norm_gain


def combine_heads(term_rows, residual, norm_gain):
    row_total = residual.shape[0]
    summed = lax.psum(term_rows(0, row_total).astype(jnp.bfloat16), "head").astype(jnp.float32)
    return layer_norm(residual.astype(jnp.float32) + summed, norm_gain).astype(jnp.bfloat16)


def build_tiles(vectors, lengths):
    holders = lengths.shape[0]
    per_holder = vectors.shape[0] // holders
    starts = (
        jnp.arange(holders, dtype=jnp.int32)[:, None] * per_holder
        + jnp.cumsum(lengths, axis=1)
        - lengths
    )
    tile_index = starts.reshape(-1)[:, None] + jnp.arange(DLMAX, dtype=jnp.int32)[None, :]
    tile_valid = jnp.arange(DLMAX)[None, :] < lengths.reshape(-1)[:, None]
    tile_index = jnp.minimum(tile_index, vectors.shape[0] - 1)
    doc_tiles = jnp.take(vectors, tile_index.reshape(-1), axis=0)
    return (doc_tiles, tile_valid)


def doc_maxima(query_rows, doc_tiles, tile_valid):
    row_count = query_rows.shape[0]
    row_block = math.gcd(row_count, 256)
    docs_here = tile_valid.shape[0]

    def block_max(block_rows):
        sims = jnp.einsum("ne,te->nt", block_rows, doc_tiles, preferred_element_type=jnp.float32)
        sims = sims.reshape(row_block, docs_here, DLMAX)
        return jnp.max(jnp.where(tile_valid[None], sims, -1e30), axis=-1)

    blocks = query_rows.reshape(row_count // row_block, row_block, query_rows.shape[1])
    return lax.map(block_max, blocks).reshape(row_count, docs_here)


def per_device(
    tokens,
    w_query,
    w_key,
    w_value,
    w_out,
    norm1_gain,
    w_inner,
    w_outer,
    norm2_gain,
    w_project,
    key_pages,
    value_pages,
    page_table,
    prompt_lengths,
    request_group,
    doc_vectors,
    doc_lengths,
    candidates,
):
    req_count, query_len, model_width = tokens.shape
    head_width = w_query.shape[1]
    heads_here = head_width // DH
    token_rows = tokens.reshape(req_count * query_len, model_width)

    def project(weight):
        out = jnp.dot(token_rows, weight, preferred_element_type=jnp.float32).astype(jnp.bfloat16)
        return out.reshape(req_count, query_len, heads_here, DH)

    queries = project(w_query)
    keys_own = project(w_key)
    values_own = project(w_value)
    score_scale = 1.0 / math.sqrt(DH)
    own_score = (
        jnp.einsum("rqhd,rkhd->rhqk", queries, keys_own, preferred_element_type=jnp.float32)
        * score_scale
    )
    row_top = jnp.max(own_score, axis=-1)
    own_weight = jnp.exp(own_score - row_top[..., None])
    row_total = jnp.sum(own_weight, axis=-1)
    weighted = jnp.einsum(
        "rhqk,rkhd->rhqd",
        own_weight.astype(jnp.bfloat16),
        values_own,
        preferred_element_type=jnp.float32,
    )
    cand_ids = lax.all_gather(candidates, "shard", axis=0, tiled=True)
    group_count = prompt_lengths.shape[0]
    page_slot = jnp.argsort(page_table)
    group_hit = request_group[:, None] == jnp.arange(group_count, dtype=jnp.int32)[None, :]
    group_len = jnp.sum(jnp.where(group_hit, prompt_lengths[None, :], 0), axis=1)
    running = (row_top, row_total, weighted)
    key_piece = lax.all_gather(key_pages, "shard", axis=0, tiled=True)
    value_piece = lax.all_gather(value_pages, "shard", axis=0, tiled=True)
    page_count = key_piece.shape[0]
    page_len = key_piece.shape[1]
    step_pages = math.gcd(page_count, max(1, 512 // page_len))
    block_count = page_count // step_pages
    key_blocks = key_piece.reshape(block_count, step_pages * page_len, heads_here, DH)
    value_blocks = value_piece.reshape(block_count, step_pages * page_len, heads_here, DH)
    slot_blocks = page_slot.reshape(block_count, step_pages)

    def one_block(state, page_block):
        old_top, old_total, old_weighted = state
        key_block, value_block, slot_block = page_block
        owner = slot_block // PPG
        offset = (slot_block % PPG)[:, None] * page_len + jnp.arange(page_len, dtype=jnp.int32)[
            None, :
        ]
        is_valid = (owner[None, :, None] == request_group[:, None, None]) & (
            offset[None] < group_len[:, None, None]
        )
        is_valid = is_valid.reshape(req_count, step_pages * page_len)
        score = (
            jnp.einsum("rqhd,khd->rhqk", queries, key_block, preferred_element_type=jnp.float32)
            * score_scale
        )
        score = jnp.where(is_valid[:, None, None, :], score, -1e30)
        new_top = jnp.maximum(old_top, jnp.max(score, axis=-1))
        fade_factor = jnp.exp(old_top - new_top)
        weight = jnp.exp(score - new_top[..., None])
        new_total = old_total * fade_factor + jnp.sum(weight, axis=-1)
        new_weighted = old_weighted * fade_factor[..., None] + jnp.einsum(
            "rhqk,khd->rhqd",
            weight.astype(jnp.bfloat16),
            value_block,
            preferred_element_type=jnp.float32,
        )
        return ((new_top, new_total, new_weighted), None)

    running, _ = lax.scan(one_block, running, (key_blocks, value_blocks, slot_blocks))
    row_top, row_total, weighted = running
    context = (weighted / row_total[..., None]).astype(jnp.bfloat16)
    context = jnp.transpose(context, (0, 2, 1, 3)).reshape(req_count * query_len, head_width)

    def attn_terms(row_start, row_count):
        return jnp.dot(context, w_out, preferred_element_type=jnp.float32)

    first = combine_heads(attn_terms, token_rows, norm1_gain)
    inner = jnp.dot(first, w_inner, preferred_element_type=jnp.float32)
    active = jax.nn.gelu(inner, approximate=False).astype(jnp.bfloat16)

    def outer_terms(row_start, row_count):
        return jnp.dot(active, w_outer, preferred_element_type=jnp.float32)

    second = combine_heads(outer_terms, first, norm2_gain)
    projected = jnp.dot(second, w_project, preferred_element_type=jnp.float32)
    embed_rows = (
        projected * lax.rsqrt(jnp.sum(projected * projected, axis=-1, keepdims=True) + 1e-06)
    ).astype(jnp.bfloat16)
    embedded = embed_rows.reshape(req_count, query_len, embed_rows.shape[1])
    doc_each = doc_lengths.shape[1]
    holder = cand_ids // doc_each
    doc_tiles, tile_valid = build_tiles(doc_vectors, doc_lengths)
    maxima = doc_maxima(
        lax.all_gather(embed_rows, "shard", axis=0, tiled=True), doc_tiles, tile_valid
    )
    docs_here = tile_valid.shape[0]
    per_doc = jnp.sum(maxima.reshape(-1, query_len, docs_here), axis=1)
    is_mine = holder == lax.axis_index(("head", "shard"))
    local_doc = cand_ids % doc_each
    doc_hit = local_doc[..., None] == jnp.arange(docs_here, dtype=jnp.int32)
    contrib = jnp.sum(jnp.where(doc_hit, per_doc[:, None, :], 0.0), axis=-1)
    contrib = jnp.where(is_mine, contrib, 0.0)
    score_part = lax.psum_scatter(contrib, "shard", scatter_dimension=0, tiled=True)
    scores = lax.psum(score_part, "head")
    return (embedded, scores)


def solution(mesh):
    in_specs = (
        P("shard", None, None),
        P(None, "head"),
        P(None, "head"),
        P(None, "head"),
        P("head", None),
        P(),
        P(None, "head"),
        P("head", None),
        P(),
        P(),
        P("shard", None, "head"),
        P("shard", None, "head"),
        P(),
        P(),
        P("shard"),
        P(("head", "shard"), None),
        P(("head", "shard"), None),
        P("shard", None),
    )
    out_specs = (P("shard", None, None), P("shard", None))
    return jax.shard_map(
        per_device, mesh=mesh, in_specs=in_specs, out_specs=out_specs, check_vma=False
    )
```

profile of v0, /device:TPU:1, one launch (start us, length us, event | category | flops | bytes accessed | tf_op | source)
XLA Modules:
  0.0 1057.8 jit_solution(1644707749141062123)
XLA Ops:
  8.8 1.4 convolution_convert_fusion.4
  10.3 1.4 convolution_convert_fusion.3
  12.6 2.5 sort.17
  15.6 132.8 %all-gather.5.cloned.1.call-done = bf16[128,64,128]{2,1,0:T(8,128)(2,1)} async-done(((bf16[2,64,128]{2,1,0:T(8,128)(2,1)}), bf16[128,64,128]{2,1,0:T(8,128)(2,1)}) %all-gather.5.cloned.1.call-update) | async-done | bytes 2097168 | tf_op jit(solution)/shard_map/all_gather | solution.py:105
  148.4 8.2 reshape.284
  156.7 10.6 %copy.80 = bf16[16,512,2,64]{1,3,2,0:T(8,128)(2,1)} copy(bf16[16,512,2,64]{3,2,1,0:T(2,128)(2,1)} %reshape.284) | data formatting | bytes 4194304 | tf_op jit(solution)/shard_map/while | solution.py:143
  167.3 121.1 %all-gather.7.cloned.1.call-done = bf16[128,64,128]{2,1,0:T(8,128)(2,1)} async-done(((bf16[2,64,128]{2,1,0:T(8,128)(2,1)}), bf16[128,64,128]{2,1,0:T(8,128)(2,1)}) %all-gather.7.cloned.1.call-update) | async-done | bytes 2097168 | tf_op jit(solution)/shard_map/all_gather | solution.py:106
  288.4 8.2 reshape.285
  296.6 10.6 copy.82
  307.2 60.7 %while.27 = (s32[]{:T(128)}, f32[4,2,64]{2,0,1:T(4,128)S(1)}, f32[4,2,64]{2,0,1:T(4,128)S(1)}, f32[4,2,64,64]{2,3,0,1:T(8,128)S(1)}, s32[16,8]{1,0:T(8,128)S(1)}...) while((s32[]{:T(128)}, f32[4,2,64]{2,0,1:T(4,128)S(1)}, ...), condition=%wide.region_7.8_spmd, body=%wide.region_4.7_spmd.sunk | while | flops 70063840 | bytes 4855253 | solution.py:143
  307.8 1.2 fusion.150
  309.5 1.4 fusion.154
  311.6 1.2 fusion.150
  313.3 1.4 fusion.154
  315.4 1.2 fusion.150
  317.1 1.4 fusion.154
  319.2 1.2 fusion.150
  320.9 1.4 fusion.154
  323.0 1.2 fusion.150
  324.7 1.4 fusion.154
  326.8 1.2 fusion.150
  328.5 1.4 fusion.154
  330.6 1.2 fusion.150
  332.3 1.4 fusion.154
  334.4 1.2 fusion.150
  336.1 1.4 fusion.154
  338.2 1.2 fusion.150
  339.9 1.4 fusion.154
  342.0 1.2 fusion.150
  343.7 1.4 fusion.154
  345.8 1.2 fusion.150
  347.5 1.4 fusion.154
  349.6 1.2 fusion.150
  351.3 1.4 fusion.154
  353.4 1.2 fusion.150
  355.1 1.4 fusion.154
  357.2 1.2 fusion.150
  358.9 1.4 fusion.154
  361.0 1.2 fusion.150
  362.7 1.4 fusion.154
  364.8 1.2 fusion.150
  366.5 1.4 fusion.154
  368.2 1.1 convolution_convert_fusion.1
  369.4 79.6 %all-reduce.4.cloned.1.call-done = bf16[256,1024]{1,0:T(8,128)(2,1)} async-done(((bf16[256,1024]{1,0:T(8,128)(2,1)}), bf16[256,1024]{1,0:T(8,128)(2,1)}) %all-reduce.4.cloned.1.call-update) | async-done | bytes 524304 | tf_op jit(solution)/shard_map/psum | solution.py:20
  449.0 1.3 fusion.27
  450.3 1.3 multiply_reduce_fusion.1
  451.9 2.7 convolution_convert_fusion
  454.8 75.4 %all-reduce.6.cloned.1.call-done = bf16[256,1024]{1,0:T(8,128)(2,1)} async-done(((bf16[256,1024]{1,0:T(8,128)(2,1)}), bf16[256,1024]{1,0:T(8,128)(2,1)}) %all-reduce.6.cloned.1.call-update) | async-done | bytes 524304 | tf_op jit(solution)/shard_map/psum | solution.py:20
  530.1 1.3 fusion.29
  531.5 1.4 multiply_reduce_fusion
  534.4 77.8 %all-gather = s32[64,4,16]{2,1,0:T(4,128)S(1)} all-gather(s32[1,4,16]{2,1,0:T(4,128)S(1)} %bitcast.140), channel_id=1, replica_groups=mesh['head'=8,'shard'=64] {'shard'}, dimensions={0}, use_global_device_ids=true | all-gather | bytes 16640 | tf_op jit(solution)/shard_map/all_gather | solution.py:99
  612.4 1.3 gather_fusion
  613.7 1.3 dynamic-slice
  615.9 57.6 %all-gather.9.cloned.1.call-done = bf16[16384,128]{1,0:T(8,128)(2,1)} async-done(((bf16[256,128]{1,0:T(8,128)(2,1)}), bf16[16384,128]{1,0:T(8,128)(2,1)}) %all-gather.9.cloned.1.call-update) | async-done | bytes 4194320 | tf_op jit(solution)/shard_map/all_gather | solution.py:168
  673.5 79.8 %while.28 = (s32[]{:T(128)}, f32[64,256,4]{1,0,2:T(8,128)S(1)}, bf16[64,256,128]{2,1,0:T(8,128)(2,1)}, bf16[512,128]{1,0:T(8,128)(2,1)S(1)}, s32[4]{0:T(128)S(1)}, /*index=5*/s32[]{:T(128)}, s32[]{:T(128)}) while((s32[]{:T(128)}, f32[64,256,4]{1,0,2:T(8,128)S(1)}, bf16[64,256,128]{2,1,0:T(8,128)(2,1)}, ...), condition=%wide.region_18.19_spmd.clone, body=%wide.region_16.18_spmd.clone.sunk | while | flops 33816064 | bytes 218721 | solution.py:50
  674.8 1.1 fusion.157
  676.0 1.1 fusion.157
  677.3 1.1 fusion.157
  681.0 1.1 fusion.157
  682.3 1.1 fusion.157
  683.5 1.1 fusion.157
  687.3 1.1 fusion.157
  753.7 220.8 %all-reduce = f32[256,16]{1,0:T(8,128)S(1)} all-reduce(f32[256,16]{1,0:T(8,128)S(1)} %copy.89), channel_id=2, replica_groups=mesh['head'=8,'shard'=64] {'shard'}, use_global_device_ids=true, to_apply=%region_21.22.clone | all-reduce | flops 4096 | bytes 32768
  974.6 76.7 %psum.23 = f32[4,16]{1,0:T(4,128)} all-reduce(f32[4,16]{1,0:T(4,128)S(1)} %constant_dynamic-slice_fusion.1), channel_id=1, replica_groups=mesh['head'=8,'shard'=64] {'head'}, use_global_device_ids=true, to_apply=%region_22.23 | all-reduce | flops 64 | bytes 512 | tf_op jit(solution)/shard_map/psum | solution.py:178
  (587 shorter events, 94.4 us)
Async XLA Ops:
  7.2 444.8 %copy-start = (bf16[512,1024]{1,0:T(8,128)(2,1)S(1)}, bf16[512,1024]{1,0:T(8,128)(2,1)}, u32[]{:S(2)}) copy-start(bf16[512,1024]{1,0:T(8,128)(2,1)} %param.29) | copy-start | bytes 3145732
  7.2 4.6 copy-start.1
  7.2 4.6 copy-start.5
  7.2 141.2 %all-gather.5.cloned.1.call-start = ((), (), s32[]{:S(2)}) async-start(), calls=%async_computation | async-start | bytes 2129920 | tf_op jit(solution)/shard_map/all_gather | solution.py:105
  7.9 280.4 %all-gather.7.cloned.1.call-start = ((), (), s32[]{:S(2)}) async-start(), calls=%async_computation.1 | async-start | bytes 2129920 | tf_op jit(solution)/shard_map/all_gather | solution.py:106
  8.7 440.3 %all-reduce.4.cloned.1.call-start = ((), (), s32[]{:S(2)}) async-start(), calls=%async_computation.2 | async-start | bytes 1048576 | tf_op jit(solution)/shard_map/psum | solution.py:20
  8.7 3.8 copy-start.12
  8.7 6.5 copy-start.13
  8.8 6.5 copy-start.14
  307.2 61.1 %copy-start.6 = (bf16[128,1024]{1,0:T(8,128)(2,1)S(1)}, bf16[128,1024]{1,0:T(8,128)(2,1)}, u32[]{:S(2)}) copy-start(bf16[128,1024]{1,0:T(8,128)(2,1)} %param.26) | copy-start | bytes 786436
  367.9 83.7 %copy-start.7 = (f32[1024]{0:T(1024)S(1)}, f32[1024]{0:T(1024)}, u32[]{:S(2)}) copy-start(f32[1024]{0:T(1024)} %param.27) | copy-start | bytes 12292
  369.3 82.6 %copy-start.9 = (bf16[1024,512]{1,0:T(8,128)(2,1)S(1)}, bf16[1024,512]{1,0:T(8,128)(2,1)}, u32[]{:S(2)}) copy-start(bf16[1024,512]{1,0:T(8,128)(2,1)} %param.28) | copy-start | bytes 3145732
  369.4 160.8 %all-reduce.6.cloned.1.call-start = ((), (), s32[]{:S(2)}) async-start(), calls=%async_computation.3 | async-start | bytes 1048576 | tf_op jit(solution)/shard_map/psum | solution.py:20
  449.0 2.7 copy-start.3
  454.7 78.2 %copy-start.10 = (bf16[1024,128]{1,0:T(8,128)(2,1)S(1)}, bf16[1024,128]{1,0:T(8,128)(2,1)}, u32[]{:S(2)}) copy-start(bf16[1024,128]{1,0:T(8,128)(2,1)} %param.31) | copy-start | bytes 786436
  454.7 78.2 %copy-start.11 = (f32[1024]{0:T(1024)S(1)}, f32[1024]{0:T(1024)}, u32[]{:S(2)}) copy-start(f32[1024]{0:T(1024)} %param.30) | copy-start | bytes 12292
  454.7 79.5 %copy-start.15 = (s32[1,4]{1,0:T(1,128)S(1)}, s32[1,4]{1,0:T(1,128)}, u32[]{:S(2)}) copy-start(s32[1,4]{1,0:T(1,128)} %param.38) | copy-start | bytes 52
  454.7 79.7 %copy-start.8 = (s32[4,16]{1,0:T(4,128)S(1)}, s32[4,16]{1,0:T(4,128)}, u32[]{:S(2)}) copy-start(s32[4,16]{1,0:T(4,128)} %param.39) | copy-start | bytes 772
  454.7 218.8 %all-gather.9.cloned.1.call-start = ((), (), s32[]{:S(2)}) async-start(), calls=%async_computation.4 | async-start | bytes 4259840 | tf_op jit(solution)/shard_map/all_gather | solution.py:168
  530.1 2.7 copy-start.4
  531.5 80.9 %copy-start.2 = (bf16[256,128]{1,0:T(8,128)(2,1)S(1)}, bf16[256,128]{1,0:T(8,128)(2,1)}, u32[]{:S(2)}) copy-start(bf16[256,128]{1,0:T(8,128)(2,1)} %param.37) | copy-start | bytes 196612
Sparse Core Ops, SparseCore 0:
  11.0 137.4 all-gather.4
  151.4 136.9 all-gather.6
  369.5 79.4 all-reduce.3
  454.8 75.2 all-reduce.5
  534.3 139.1 all-gather.8
where the time goes:
time: 1060 us
  waiting for transfers between devices  468 us (44%)
  blocking collectives  375 us (35%)
  matrix products  118 us (11%)
  local copies, waits for them, and re-layouts  51.2 us (5%)
  other arithmetic  26.6 us (3%)
  between operations  14.8 us (1%)
    unnamed x1, blocking collectives  221 us
    psum x2, waiting for transfers between devices, combine_heads(): lax.psum(term_rows(0, row_total).astype(jnp.bfloat16), 'head')  155 us
    all_gather x1, waiting for transfers between devices, per_device(): key_piece = lax.all_gather(key_pages, 'shard', axis=0, tiled=True)  133 us
    all_gather x1, waiting for transfers between devices, per_device(): value_piece = lax.all_gather(value_pages, 'shard', axis=0, tiled=True)  121 us
    all_gather x1, blocking collectives, per_device(): cand_ids = lax.all_gather(candidates, 'shard', axis=0, tiled=True)  77.8 us
    psum x1, blocking collectives, per_device(): scores = lax.psum(score_part, 'head')  76.7 us
    dot_general x64, matrix products, block_max(): jnp.einsum('ne,te->nt', block_rows, doc_tiles, preferred_element_type=jnp...  69.4 us
    all_gather x1, waiting for transfers between devices, per_device(): lax.all_gather(embed_rows, 'shard', axis=0, tiled=True)  57.6 us
  transfers between devices with their start and end apart: 5, of which 5 were waited for; matrix products, arithmetic and copies ran while one was open for 3% of the time, Pallas kernels for 0%

commit v1 on v0

--- a/solution.py
+++ b/solution.py
@@ -165,7 +165,11 @@
     holder = cand_ids // doc_each
     doc_tiles, tile_valid = build_tiles(doc_vectors, doc_lengths)
     maxima = doc_maxima(
-        lax.all_gather(embed_rows, "shard", axis=0, tiled=True), doc_tiles, tile_valid
+        jnp.concatenate(
+            lax.all_to_all(jnp.stack([embed_rows] * lax.axis_size("shard")), "shard", 0, 0), axis=0
+        ),
+        doc_tiles,
+        tile_valid,
     )
     docs_here = tile_valid.shape[0]
     per_doc = jnp.sum(maxima.reshape(-1, query_len, docs_here), axis=1)

time: 1060 us -> 1210 us (1.14)
  blocking collectives: 375 us -> 566 us
  waiting for transfers between devices: 468 us -> 410 us
  starting transfers between devices: 0.2 us -> 15.4 us
    all_gather x1, blocking collectives: 77.8 us -> 249 us  [per_device(): cand_ids = lax.all_gather(candidates, 'shard', axis=0, tiled=True)]
    all_gather x1 -> x0, waiting for transfers between devices: 57.6 us -> none  [per_device(): lax.all_gather(embed_rows, 'shard', axis=0, tiled=True)]
    psum x1, blocking collectives: 76.7 us -> 94.1 us  [per_device(): scores = lax.psum(score_part, 'head')]
    all_to_all x0 -> x1, starting transfers between devices: none -> 15.2 us  [per_device(): lax.all_to_all(jnp.stack([embed_rows] * lax.axis_size('shard')), 'shard',...]
  transfers between devices with their start and end apart: 5 -> 5, of which waited for: 5 -> 4; matrix products, arithmetic and copies ran while one was open for 3% -> 2% of each run, Pallas kernels for 0% -> 0%
where the time goes in v1:
time: 1210 us
  blocking collectives  566 us (47%)
  waiting for transfers between devices  410 us (34%)
  matrix products  118 us (10%)
  local copies, waits for them, and re-layouts  54.2 us (4%)
  other arithmetic  26 us (2%)
  starting transfers between devices  15.4 us (1%)
  between operations  14.8 us (1%)
    all_gather x1, blocking collectives, per_device(): cand_ids = lax.all_gather(candidates, 'shard', axis=0, tiled=True)  249 us
    unnamed x1, blocking collectives  222 us
    psum x2, waiting for transfers between devices, combine_heads(): lax.psum(term_rows(0, row_total).astype(jnp.bfloat16), 'head')  155 us
    all_gather x1, waiting for transfers between devices, per_device(): key_piece = lax.all_gather(key_pages, 'shard', axis=0, tiled=True)  133 us
    all_gather x1, waiting for transfers between devices, per_device(): value_piece = lax.all_gather(value_pages, 'shard', axis=0, tiled=True)  121 us
    psum x1, blocking collectives, per_device(): scores = lax.psum(score_part, 'head')  94.1 us
    dot_general x64, matrix products, block_max(): jnp.einsum('ne,te->nt', block_rows, doc_tiles, preferred_element_type=jnp...  69.4 us
  transfers between devices with their start and end apart: 5, of which 4 were waited for; matrix products, arithmetic and copies ran while one was open for 2% of the time, Pallas kernels for 0%

profile of v1, /device:TPU:1, one launch (start us, length us, event | category | flops | bytes accessed | tf_op | source)
XLA Modules:
  0.0 1207.9 jit_solution(15664598387911425527)
XLA Ops:
  8.8 1.4 convolution_convert_fusion.4
  10.3 1.4 convolution_convert_fusion.3
  12.6 2.5 sort.17
  15.6 132.8 %all-gather.4.cloned.1.call-done = bf16[128,64,128]{2,1,0:T(8,128)(2,1)} async-done(((bf16[2,64,128]{2,1,0:T(8,128)(2,1)}), bf16[128,64,128]{2,1,0:T(8,128)(2,1)}) %all-gather.4.cloned.1.call-update) | async-done | bytes 2097168 | tf_op jit(solution)/shard_map/all_gather | solution.py:105
  148.4 8.2 reshape.282
  156.7 10.6 copy.80
  167.3 121.1 %all-gather.6.cloned.1.call-done = bf16[128,64,128]{2,1,0:T(8,128)(2,1)} async-done(((bf16[2,64,128]{2,1,0:T(8,128)(2,1)}), bf16[128,64,128]{2,1,0:T(8,128)(2,1)}) %all-gather.6.cloned.1.call-update) | async-done | bytes 2097168 | tf_op jit(solution)/shard_map/all_gather | solution.py:106
  288.4 8.2 reshape.283
  296.6 10.6 copy.82
  307.2 60.7 %while.27 = (s32[]{:T(128)}, f32[4,2,64]{2,0,1:T(4,128)S(1)}, f32[4,2,64]{2,0,1:T(4,128)S(1)}, f32[4,2,64,64]{2,3,0,1:T(8,128)S(1)}, s32[16,8]{1,0:T(8,128)S(1)}...) while((s32[]{:T(128)}, f32[4,2,64]{2,0,1:T(4,128)S(1)}, ...), condition=%wide.region_7.8_spmd, body=%wide.region_4.7_spmd.sunk | while | flops 70063840 | bytes 4855253 | solution.py:143
  307.8 1.2 fusion.150
  309.5 1.4 fusion.154
  311.6 1.2 fusion.150
  313.3 1.4 fusion.154
  315.4 1.2 fusion.150
  317.1 1.4 fusion.154
  319.2 1.2 fusion.150
  320.9 1.4 fusion.154
  323.0 1.2 fusion.150
  324.7 1.4 fusion.154
  326.8 1.2 fusion.150
  328.5 1.4 fusion.154
  330.6 1.2 fusion.150
  332.3 1.4 fusion.154
  334.4 1.2 fusion.150
  336.1 1.4 fusion.154
  338.2 1.2 fusion.150
  339.9 1.4 fusion.154
  342.0 1.2 fusion.150
  343.7 1.4 fusion.154
  345.8 1.2 fusion.150
  347.5 1.4 fusion.154
  349.6 1.2 fusion.150
  351.3 1.4 fusion.154
  353.4 1.2 fusion.150
  355.1 1.4 fusion.154
  357.2 1.2 fusion.150
  358.9 1.4 fusion.154
  361.0 1.2 fusion.150
  362.7 1.4 fusion.154
  364.8 1.2 fusion.150
  366.5 1.4 fusion.154
  368.2 1.1 convolution_convert_fusion.1
  369.4 79.6 %all-reduce.4.cloned.1.call-done = bf16[256,1024]{1,0:T(8,128)(2,1)} async-done(((bf16[256,1024]{1,0:T(8,128)(2,1)}), bf16[256,1024]{1,0:T(8,128)(2,1)}) %all-reduce.4.cloned.1.call-update) | async-done | bytes 524304 | tf_op jit(solution)/shard_map/psum | solution.py:20
  449.0 1.3 fusion.27
  450.3 1.3 multiply_reduce_fusion.1
  451.9 2.7 convolution_convert_fusion
  454.7 75.5 %all-reduce.6.cloned.1.call-done = bf16[256,1024]{1,0:T(8,128)(2,1)} async-done(((bf16[256,1024]{1,0:T(8,128)(2,1)}), bf16[256,1024]{1,0:T(8,128)(2,1)}) %all-reduce.6.cloned.1.call-update) | async-done | bytes 524304 | tf_op jit(solution)/shard_map/psum | solution.py:20
  530.1 1.3 fusion.29
  531.5 1.3 multiply_reduce_fusion
  533.5 3.0 stack.2
  536.5 15.2 %all-to-all-start = ((bf16[64,256,128]{2,1,0:T(8,128)(2,1)}), bf16[64,256,128]{2,1,0:T(8,128)(2,1)}, u32[]{:S(2)}, u32[]{:S(2)}) async-start(bf16[64,256,128]{2,1,0:T(8,128)(2,1)} %stack.2), calls=%async_computation | async-start | bytes 8388608 | tf_op jit(solution)/shard_map/all_to_all | solution.py:169
  551.9 249.5 %all-gather = s32[64,4,16]{2,1,0:T(4,128)S(1)} all-gather(s32[1,4,16]{2,1,0:T(4,128)S(1)} %bitcast.139), channel_id=1, replica_groups=mesh['head'=8,'shard'=64] {'shard'}, dimensions={0}, use_global_device_ids=true | all-gather | bytes 16640 | tf_op jit(solution)/shard_map/all_gather | solution.py:99
  801.5 1.3 gather_fusion
  802.9 1.2 dynamic-slice
  805.0 79.8 %while.28 = (s32[]{:T(128)}, f32[64,256,4]{1,0,2:T(8,128)S(1)}, bf16[64,256,128]{2,1,0:T(8,128)(2,1)}, bf16[512,128]{1,0:T(8,128)(2,1)S(1)}, s32[4]{0:T(128)S(1)}, /*index=5*/s32[]{:T(128)}, s32[]{:T(128)}) while((s32[]{:T(128)}, f32[64,256,4]{1,0,2:T(8,128)S(1)}, bf16[64,256,128]{2,1,0:T(8,128)(2,1)}, ...), condition=%wide.region_18.19_spmd.clone, body=%wide.region_16.18_spmd.clone.sunk | while | flops 33816064 | bytes 218721 | solution.py:50
  805.1 1.1 fusion.157
  808.8 1.1 fusion.157
  810.0 1.1 fusion.157
  811.3 1.1 fusion.157
  815.0 1.1 fusion.157
  816.3 1.1 fusion.157
  885.2 222.0 %all-reduce = f32[256,16]{1,0:T(8,128)S(1)} all-reduce(f32[256,16]{1,0:T(8,128)S(1)} %copy.89), channel_id=2, replica_groups=mesh['head'=8,'shard'=64] {'shard'}, use_global_device_ids=true, to_apply=%region_21.22.clone | all-reduce | flops 4096 | bytes 32768
  1107.2 94.1 %psum.23 = f32[4,16]{1,0:T(4,128)} all-reduce(f32[4,16]{1,0:T(4,128)S(1)} %constant_dynamic-slice_fusion.1), channel_id=1, replica_groups=mesh['head'=8,'shard'=64] {'head'}, use_global_device_ids=true, to_apply=%region_22.23 | all-reduce | flops 64 | bytes 512 | tf_op jit(solution)/shard_map/psum | solution.py:182
  (589 shorter events, 94.8 us)
Async XLA Ops:
  7.2 444.8 %copy-start = (bf16[512,1024]{1,0:T(8,128)(2,1)S(1)}, bf16[512,1024]{1,0:T(8,128)(2,1)}, u32[]{:S(2)}) copy-start(bf16[512,1024]{1,0:T(8,128)(2,1)} %param.29) | copy-start | bytes 3145732
  7.2 4.6 copy-start.1
  7.2 4.6 copy-start.6
  7.2 141.2 %all-gather.4.cloned.1.call-start = ((), (), s32[]{:S(2)}) async-start(), calls=%async_computation.1 | async-start | bytes 2129920 | tf_op jit(solution)/shard_map/all_gather | solution.py:105
  7.9 280.4 %all-gather.6.cloned.1.call-start = ((), (), s32[]{:S(2)}) async-start(), calls=%async_computation.2 | async-start | bytes 2129920 | tf_op jit(solution)/shard_map/all_gather | solution.py:106
  8.7 440.3 %all-reduce.4.cloned.1.call-start = ((), (), s32[]{:S(2)}) async-start(), calls=%async_computation.3 | async-start | bytes 1048576 | tf_op jit(solution)/shard_map/psum | solution.py:20
  8.7 3.8 copy-start.13
  8.7 6.5 copy-start.14
  8.8 6.5 copy-start.15
  307.2 61.1 %copy-start.7 = (bf16[128,1024]{1,0:T(8,128)(2,1)S(1)}, bf16[128,1024]{1,0:T(8,128)(2,1)}, u32[]{:S(2)}) copy-start(bf16[128,1024]{1,0:T(8,128)(2,1)} %param.26) | copy-start | bytes 786436
  367.9 83.7 %copy-start.8 = (f32[1024]{0:T(1024)S(1)}, f32[1024]{0:T(1024)}, u32[]{:S(2)}) copy-start(f32[1024]{0:T(1024)} %param.27) | copy-start | bytes 12292
  369.3 82.6 %copy-start.10 = (bf16[1024,512]{1,0:T(8,128)(2,1)S(1)}, bf16[1024,512]{1,0:T(8,128)(2,1)}, u32[]{:S(2)}) copy-start(bf16[1024,512]{1,0:T(8,128)(2,1)} %param.28) | copy-start | bytes 3145732
  369.4 160.8 %all-reduce.6.cloned.1.call-start = ((), (), s32[]{:S(2)}) async-start(), calls=%async_computation.4 | async-start | bytes 1048576 | tf_op jit(solution)/shard_map/psum | solution.py:20
  449.0 2.7 copy-start.3
  454.7 78.2 %copy-start.11 = (bf16[1024,128]{1,0:T(8,128)(2,1)S(1)}, bf16[1024,128]{1,0:T(8,128)(2,1)}, u32[]{:S(2)}) copy-start(bf16[1024,128]{1,0:T(8,128)(2,1)} %param.31) | copy-start | bytes 786436
  454.7 78.2 %copy-start.12 = (f32[1024]{0:T(1024)S(1)}, f32[1024]{0:T(1024)}, u32[]{:S(2)}) copy-start(f32[1024]{0:T(1024)} %param.30) | copy-start | bytes 12292
  530.1 2.7 copy-start.4
  533.5 3.0 copy-start.5
  536.5 15.3 %copy-start.16 = (s32[1,4]{1,0:T(1,128)S(1)}, s32[1,4]{1,0:T(1,128)}, u32[]{:S(2)}) copy-start(s32[1,4]{1,0:T(1,128)} %param.38) | copy-start | bytes 52
  536.5 15.4 %copy-start.9 = (s32[4,16]{1,0:T(4,128)S(1)}, s32[4,16]{1,0:T(4,128)}, u32[]{:S(2)}) copy-start(s32[4,16]{1,0:T(4,128)} %param.39) | copy-start | bytes 772
  536.5 265.1 %copy-start.2 = (bf16[256,128]{1,0:T(8,128)(2,1)S(1)}, bf16[256,128]{1,0:T(8,128)(2,1)}, u32[]{:S(2)}) copy-start(bf16[256,128]{1,0:T(8,128)(2,1)} %param.37) | copy-start | bytes 196612
  536.5 268.5 %all-to-all-start = ((bf16[64,256,128]{2,1,0:T(8,128)(2,1)}), bf16[64,256,128]{2,1,0:T(8,128)(2,1)}, u32[]{:S(2)}, u32[]{:S(2)}) async-start(bf16[64,256,128]{2,1,0:T(8,128)(2,1)} %stack.2), calls=%async_computation | async-start | bytes 8388608 | tf_op jit(solution)/shard_map/all_to_all | solution.py:169
Sparse Core Ops, SparseCore 0:
  11.0 137.4 all-gather.3
  151.4 136.9 all-gather.5
  369.5 79.4 all-reduce.3
  454.8 75.2 all-reduce.5
